TPU v7x, 32 devices: a whole 2x2x4 slice. The times are simulated.
32 devices in a mesh: lat: 4 (over x, core), lon: 8 (over z, y).
Axes of the slice: x: 2, y: 2, z: 4, core: 2. Of those that a mesh axis runs over, the one named last changes fastest.
Arguments:
- northward_volume_flux: bfloat16 [75, 1024, 1024], P(None, 'lat', 'lon'), may hold values from -6 to 6
- sheet_warmth: bfloat16 [75, 1024, 1024], P(None, 'lat', 'lon'), may hold values from -6 to 6
- ocean_region_ids: int32 [1024, 1024], P('lat', 'lon'), may hold values from 0 to 4
- ocean_grid_flags: int32 [1024, 1024], P('lat', 'lon'), may hold values 0 or 1
- thick_sheet_tally: int32 [1024, 1024], P('lat', 'lon'), may hold values from 1 to 75
Outputs:
- stream_layers: float32 [5, 75, 1024], P(None, None, 'lat')
- stream_north: float32 [5, 75, 1024], P(None, None, 'lat')
- heat_layers: float32 [5, 75, 1024], P(None, None, 'lat')
All inputs are finite; a program needn't handle non-finite values. No bound on the sum of `ocean_grid_flags` on one device may be relied on, other than what follows from the above.
Results may differ from a plain program's by a relative error of at most 0.0003.
Values may be sent and summed in bfloat16 or wider, within the bound.
A program may use at most 64 MiB of HBM per device.

v0:
```python
import math

import jax
import jax.numpy as jnp
from jax import lax
from jax.sharding import PartitionSpec as P

BASINS = 5


def from_behind(x, axis, by):
    size = lax.axis_size(axis)
    pairs = [(i, i + by) for i in range(size) if 0 <= i + by < size]
    return lax.ppermute(x, axis, pairs)


def on_device(
    northward_volume_flux, sheet_warmth, ocean_region_ids, ocean_grid_flags, thick_sheet_tally
):
    layers, rows, columns = northward_volume_flux.shape
    northerly_strip = from_behind(sheet_warmth[:, :1, :], "lat", -1)
    centre_warmth = sheet_warmth.astype(jnp.float32)
    upper_neighbour = jnp.concatenate(
        [centre_warmth[:, 1:, :], northerly_strip.astype(jnp.float32)], axis=1
    )
    interface_warmth = 0.5 * (centre_warmth + upper_neighbour)
    level = jnp.arange(layers, dtype=jnp.int32)[:, None, None]
    live_cells = ocean_grid_flags[None].astype(jnp.float32) * (
        level < thick_sheet_tally[None]
    ).astype(jnp.float32)
    flow = northward_volume_flux.astype(jnp.float32) * live_cells
    basin_table = (
        ocean_region_ids[:, :, None] == jnp.arange(BASINS, dtype=jnp.int32)[None, None, :]
    ).astype(jnp.float32)
    scale_x = 1.0 / math.sqrt(columns * lax.axis_size("lon"))
    scale_layers = 1.0 / math.sqrt(layers)
    scale_y = 1.0 / math.sqrt(rows * lax.axis_size("lat"))
    zonal_part = (
        jnp.einsum("kyx,yxb->bky", flow, basin_table, precision=lax.Precision.HIGHEST) * scale_x
    )
    heat_part = (
        jnp.einsum(
            "kyx,yxb->bky", flow * interface_warmth, basin_table, precision=lax.Precision.HIGHEST
        )
        * scale_x
    )
    zonal_flow, heat_layers = lax.psum((zonal_part, heat_part), "lon")
    stream_layers = jnp.cumsum(zonal_flow, axis=1) * scale_layers
    running = jnp.cumsum(stream_layers, axis=2)
    totals = running[:, :, -1]
    every = lax.all_gather(totals[None], "lat", axis=0, tiled=True)
    lower = (jnp.arange(every.shape[0], dtype=jnp.int32) < lax.axis_index("lat")).astype(
        jnp.float32
    )
    carried = jnp.sum(every * lower[:, None, None], axis=0)
    stream_north = (running + carried[:, :, None]) * scale_y
    return (stream_layers, stream_north, heat_layers)


def solution(mesh):
    placed = (
        P(None, "lat", "lon"),
        P(None, "lat", "lon"),
        P("lat", "lon"),
        P("lat", "lon"),
        P("lat", "lon"),
    )
    return jax.shard_map(
        on_device,
        mesh=mesh,
        in_specs=placed,
        out_specs=(P(None, None, "lat"), P(None, None, "lat"), P(None, None, "lat")),
        check_vma=False,
    )
```

profile of v0, /device:TPU:0, one launch (start us, length us, event | category | flops | bytes accessed | tf_op | source)
XLA Modules:
  0.0 180.3 jit_solution(14437243361531758981)
XLA Ops:
  7.2 0.0 all-reduce.3.cloned.1.call-start
  7.2 0.0 slice-start
  7.2 1.1 slice.19
  8.3 0.0 copy-start.4
  8.3 0.0 slice-start.1
  8.3 0.0 copy-start.3
  8.3 1.4 collective-permute-start
  9.8 8.1 %slice.23 = f32[75,255,128]{2,1,0:T(8,128)} slice(bf16[75,256,128]{2,1,0:T(8,128)(2,1)} %param.6), slice={[0:75], [1:256], [0:128]} | slice | bytes 19584000 | tf_op jit(solution)/shard_map/slice | solution.py:24
  17.9 0.0 copy-done.4
  17.9 0.0 collective-permute-done
  17.9 0.0 slice-done
  17.9 0.0 slice-done.1
  17.9 0.0 copy-done.3
  18.0 0.0 copy-start.2
  18.0 7.5 %fusion.5 = (f32[75,256,128]{2,1,0:T(8,128)S(1)}, f32[75,256,128]{2,1,0:T(8,128)S(1)}) fusion(f32[75,1,128]{2,1,0:T(1,128)S(1)} %convert_element_type.26, f32[75,255,128]{2,1,0:T(8,128)} %slice.23, bf16[75,256,128]{2,1,0:T(8,128)(2,1)S(1)} %bitcast.5, f32[256,128]{1,0:T(8,128)S(1)} %convert_element_type.23, s32[256,128]{1,0:T(8,128)S(1)} %copy-done.3, ...), kind=kLoop, calls=%fused_computation.6 | loop fusion | flops 22118400 | bytes 39583744 | tf_op jit(solution)/shard_map/mul | solution.py:43
  25.5 0.0 copy-done.2
  25.5 13.9 %fusion.15 = f32[5,75,256]{1,0,2:T(8,128)} fusion(f32[75,256,128]{2,1,0:T(8,128)S(1)} %get-tuple-element.14, s32[256,128]{1,0:T(8,128)S(1)} %copy-done.2), kind=kOutput, calls=%fused_computation.12 | convolution fusion | flops 147715840 | bytes 10345472 | tf_op jit(solution)/shard_map/kyx,yxb->bky/dot_general | solution.py:42
  39.3 14.1 %fusion.9 = f32[5,75,256]{1,0,2:T(8,128)} fusion(f32[75,256,128]{2,1,0:T(8,128)S(1)} %get-tuple-element.15, s32[256,128]{1,0:T(8,128)S(1)} %copy-done.2), kind=kOutput, calls=%fused_computation.10 | convolution fusion | flops 147715840 | bytes 10345472 | tf_op jit(solution)/shard_map/kyx,yxb->bky/dot_general | solution.py:39
  53.4 0.0 all-reduce.3.cloned.1.call-update
  53.5 106.0 %all-reduce.3.cloned.1.call-done = (f32[5,75,256]{1,0,2:T(8,128)}, f32[5,75,256]{1,0,2:T(8,128)}) async-done(((f32[5,75,256]{1,0,2:T(8,128)}, f32[5,75,256]{1,0,2:T(8,128)}), (f32[5,75,256]{1,0,2:T(8,128)}, f32[5,75,256]{1,0,2:T(8,128)})) %all-reduce.3.cloned.1.call-update) | async-done | bytes 768016 | tf_op jit(solution)/shard_map/psum | solution.py:47
  159.4 0.0 copy-start.1
  159.4 1.6 copy.20
  161.0 0.4 reduce_window_sum.26
  161.4 0.0 copy-start
  161.4 0.2 mul.60
  161.7 3.1 %reduce-window.6 = f32[5,75,2,128]{3,1,2,0:T(8,128)S(1)} reduce-window(f32[5,75,2,128]{3,1,2,0:T(8,128)S(1)} %copy.21, f32[]{:T(128)} %constant.8.clone.1), window={size=1x1x1x128 pad=0_0x0_0x0_0x127_0}, to_apply=%region_2.0 | reduce-window | flops 12192000 | bytes 768004 | tf_op jit(solution)/shard_map/reduce-window
  164.8 0.4 slice_reduce_fusion
  165.2 0.2 broadcast_add_fusion
  165.4 0.2 copy.22
  165.6 0.3 reduce_window_sum.28
  165.9 0.1 slice.22
  166.0 0.1 copy.23
  166.2 5.2 %all-gather = f32[20,75,1]{1,2,0:T(1,128)S(1)} all-gather(f32[5,75,1]{1,2,0:T(1,128)S(1)} %copy.23), channel_id=2, replica_groups=mesh['lat'=4,'lon'=8] {'lat'}, dimensions={0}, use_global_device_ids=true | all-gather | bytes 7500 | tf_op jit(solution)/shard_map/all_gather | solution.py:51
  171.4 0.1 multiply_reduce_fusion
  171.5 0.9 add_multiply_fusion
  172.4 0.0 copy-done.1
  172.4 1.1 copy.25
  173.4 0.0 copy-done
  (10 shorter events, 0.2 us)
Async XLA Ops:
  7.2 152.3 %all-reduce.3.cloned.1.call-start = ((), (), s32[]{:S(2)}) async-start(), calls=%async_computation | async-start | bytes 4194304 | tf_op jit(solution)/shard_map/psum | solution.py:47
  7.2 10.7 %slice-start = ((s8[4915200]{0:T(1024)(128)(4,1)}), s8[4194304]{0:T(1024)(128)(4,1)S(1)}, s32[]{:S(2)}) async-start(s8[4915200]{0:T(1024)(128)(4,1)} %bitcast.4), calls=%async_computation.1 | async-start | bytes 8388608
  8.3 9.5 %copy-start.4 = (s32[256,128]{1,0:T(8,128)S(1)}, s32[256,128]{1,0:T(8,128)}, u32[]{:S(2)}) copy-start(s32[256,128]{1,0:T(8,128)} %param.8) | copy-start | bytes 393220
  8.3 9.6 %slice-start.1 = ((s8[4915200]{0:T(1024)(128)(4,1)}), s8[720896]{0:T(1024)(128)(4,1)S(1)}, s32[]{:S(2)}) async-start(s8[4915200]{0:T(1024)(128)(4,1)} %bitcast.4), calls=%async_computation.2 | async-start | bytes 1441792
  8.3 9.6 %copy-start.3 = (s32[256,128]{1,0:T(8,128)S(1)}, s32[256,128]{1,0:T(8,128)}, u32[]{:S(2)}) copy-start(s32[256,128]{1,0:T(8,128)} %param.9) | copy-start | bytes 393220
  8.3 9.5 %collective-permute-start = (bf16[75,1,128]{2,1,0:T(2,128)(2,1)S(1)}, bf16[75,1,128]{2,1,0:T(2,128)(2,1)S(1)}, u32[]{:S(2)}, u32[]{:S(2)}) collective-permute-start(bf16[75,1,128]{2,1,0:T(2,128)(2,1)S(1)} %slice.19), channel_id=1, source_target_pairs={{8,0},{16,8},{24,16},{9,1},{17,9},{25,17},{10,2},{18,10},{26,18},{... | collective-permute-start | bytes 57608 | tf_op jit(solution)/shard_map/ppermute | solution.py:14
  18.0 7.5 %copy-start.2 = (s32[256,128]{1,0:T(8,128)S(1)}, s32[256,128]{1,0:T(8,128)}, u32[]{:S(2)}) copy-start(s32[256,128]{1,0:T(8,128)} %param.7) | copy-start | bytes 393220
  159.4 12.9 %copy-start.1 = (f32[5,75,256]{1,0,2:T(8,128)S(1)}, f32[5,75,256]{1,0,2:T(8,128)}, u32[]{:S(2)}) copy-start(f32[5,75,256]{1,0,2:T(8,128)} %get-tuple-element.13) | copy-start | bytes 1152004
  161.4 12.0 %copy-start = (f32[5,75,256]{2,1,0:T(8,128)}, f32[5,75,256]{2,1,0:T(8,128)S(1)}, u32[]{:S(2)}) copy-start(f32[5,75,256]{2,1,0:T(8,128)S(1)} %broadcast_multiply_fusion) | copy-start | bytes 1152004
Sparse Core Ops, SparseCore 0:
  53.6 105.8 all-reduce.2
where the time goes:
time: 180 us
  waiting for transfers between devices  106 us (59%)
  matrix products  27.9 us (16%)
  between operations  14.3 us (8%)
  local copies, waits for them, and re-layouts  13.2 us (7%)
  other arithmetic  12.2 us (7%)
  blocking collectives  5.2 us (3%)
    psum x1, waiting for transfers between devices, on_device(): zonal_flow, heat_layers = lax.psum((zonal_part, heat_part), 'lon')  106 us
    dot_general x1, matrix products, on_device(): jnp.einsum('kyx,yxb->bky', flow, basin_table, precision=lax.Precision.HIG...  14.1 us
    dot_general x1, matrix products, on_device(): jnp.einsum('kyx,yxb->bky', flow * interface_warmth, basin_table, precisio...  13.9 us
    slice x1, local copies, waits for them, and re-layouts, on_device(): centre_warmth[:, 1:, :]  8.07 us
    mul x1, other arithmetic, on_device(): flow * interface_warmth  7.49 us
    all_gather x1, blocking collectives, on_device(): every = lax.all_gather(totals[None], 'lat', axis=0, tiled=True)  5.2 us
  transfers between devices with their start and end apart: 2, of which 1 were waited for; matrix products, arithmetic and copies ran while one was open for 4% of the time, Pallas kernels for 0%

commit v1 on v0

v1 whole, which is shorter than its diff:
```python
import functools
import math

import jax
import jax.numpy as jnp
from jax import lax
from jax.experimental import pallas as pl
from jax.experimental.pallas import tpu as pltpu
from jax.sharding import PartitionSpec as P

BASINS = 5
GROUP = 8
F32, BF16 = jnp.float32, jnp.bfloat16


def nt_dot(a, b):
    return lax.dot_general(a, b, (((1,), (1,)), ((), ())), preferred_element_type=F32)


def split(x):
    high = x.astype(BF16)
    return high, (x - high.astype(F32)).astype(BF16)


def kernel(
    n_lat, n_lon, layers, scales,
    flux_hbm, warm_hbm, ids_ref, flags_ref, tally_ref,
    stream_out, north_out, heat_out,
    flux, warm, masks, live_tally, acc, landed, reduced, strip, zonal, totals, every,
    in_sem, rs_send, rs_recv, ag_send, ag_recv, strip_send, strip_recv, tot_send, tot_recv,
):
    scale_x, scale_layers, scale_y = scales
    rows, columns = ids_ref.shape
    groups = flux.shape[0] // GROUP
    planes = 2 * BASINS
    depth = landed.shape[1]
    me_lat = lax.axis_index("lat")
    me = lax.axis_index("lon")

    loads = []
    for g in range(groups):
        size = min(GROUP, layers - g * GROUP)
        part = pl.ds(g * GROUP, size)
        pair = (
            pltpu.make_async_copy(flux_hbm.at[part], flux.at[part], in_sem.at[0, g]),
            pltpu.make_async_copy(warm_hbm.at[part], warm.at[part], in_sem.at[1, g]),
        )
        for copy in pair:
            copy.start()
        loads.append(pair)

    barrier = pltpu.get_barrier_semaphore()
    for j in range(1, n_lon):
        pl.semaphore_signal(
            barrier, inc=1, device_id={"lon": lax.rem(me + j, n_lon)},
            device_id_type=pl.DeviceIdType.MESH,
        )
    for j in range(1, n_lat):
        pl.semaphore_signal(
            barrier, inc=1, device_id={"lat": lax.rem(me_lat + j, n_lat)},
            device_id_type=pl.DeviceIdType.MESH,
        )

    spare = groups * GROUP - layers
    if spare:
        flux[pl.ds(layers, spare)] = jnp.zeros((spare, rows, columns), BF16)
        warm[pl.ds(layers, spare)] = jnp.zeros((spare, rows, columns), BF16)
    left = acc.shape[0] - groups * planes
    if left:
        acc[pl.ds(groups * planes, left)] = jnp.zeros((left, GROUP, rows), F32)
    ids = ids_ref[...]
    for b in range(BASINS):
        masks[b] = (ids == b).astype(F32).astype(BF16)
    live_tally[...] = flags_ref[...] * tally_ref[...]

    pl.semaphore_wait(barrier, n_lon - 1 + n_lat - 1)
    strip_copy = pltpu.make_async_remote_copy(
        src_ref=warm_hbm.at[:, pl.ds(0, 8), :], dst_ref=strip,
        send_sem=strip_send, recv_sem=strip_recv,
        device_id={"lat": lax.rem(me_lat + n_lat - 1, n_lat)},
        device_id_type=pl.DeviceIdType.MESH,
    )
    pl.when(me_lat > 0)(strip_copy.start)

    last_row = lax.broadcasted_iota(jnp.int32, (rows, columns), 0) == rows - 1
    lane_half = lax.broadcasted_iota(jnp.int32, (GROUP, 2 * columns), 1) // columns
    slot = lax.broadcasted_iota(jnp.int32, (GROUP, 2 * columns), 0)

    def one_group(g, carry):
        zsum = [jnp.zeros((GROUP, rows), F32) for _ in range(BASINS)]
        hsum = [jnp.zeros((GROUP, rows), F32) for _ in range(BASINS)]
        for pair in range(GROUP // 2):
            held = []
            for half in range(2):
                i = 2 * pair + half
                k = g * GROUP + i
                live = k < live_tally[...]
                f = jnp.where(live, flux[k].astype(F32), 0.0)
                t = warm[k].astype(F32)
                up = jnp.where(last_row, 0.0, pltpu.roll(t, rows - 1, 0))
                high, low = split(f * (t + up))
                fb = f.astype(BF16)
                held.append(fb)
                pick = (slot == i).astype(F32).astype(BF16)
                for b in range(BASINS):
                    m = masks[b]
                    hsum[b] += nt_dot(pick, jnp.concatenate([high * m, low * m], axis=1))
            pick = (slot == 2 * pair + lane_half).astype(F32).astype(BF16)
            for b in range(BASINS):
                m = masks[b]
                zsum[b] += nt_dot(pick, jnp.concatenate([held[0] * m, held[1] * m], axis=1))
        for b in range(BASINS):
            acc[g * planes + b] = zsum[b] * scale_x
            acc[g * planes + BASINS + b] = hsum[b] * (0.5 * scale_x)
        return carry

    for pair in loads:
        for copy in pair:
            copy.wait()
    lax.fori_loop(0, groups, one_group, 0)

    @pl.when(me_lat < n_lat - 1)
    def _():
        strip_copy.wait_recv()
        near = strip[...].astype(F32)[:, 0, :]
        mine = flux[pl.ds(0, layers), pl.ds(rows - 16, 16), :].astype(F32)[:, 15, :]
        level = lax.broadcasted_iota(jnp.int32, (layers, columns), 0)
        tall = live_tally[pl.ds(rows - 1, 1), :]
        extra = jnp.where(level < tall, near * mine, 0.0) * (0.5 * scale_x)
        last = ids_ref[pl.ds(rows - 1, 1), :]
        end = lax.broadcasted_iota(jnp.int32, (GROUP, rows), 1) == rows - 1
        for b in range(BASINS):
            column = jnp.sum(jnp.where(last == b, extra, 0.0), axis=1, keepdims=True)
            if spare:
                column = jnp.concatenate([column, jnp.zeros((spare, 1), F32)], axis=0)
            for g in range(groups):
                at = g * planes + BASINS + b
                piece = column[g * GROUP:(g + 1) * GROUP]
                acc[at] = acc[at] + jnp.where(end, piece, 0.0)

    def to_lon(peer, src, dst, send, recv):
        return pltpu.make_async_remote_copy(
            src_ref=src, dst_ref=dst, send_sem=send, recv_sem=recv,
            device_id={"lon": peer}, device_id_type=pl.DeviceIdType.MESH,
        )

    scatter = []
    for j in range(1, n_lon):
        peer = lax.rem(me + j, n_lon)
        copy = to_lon(
            peer, acc.at[pl.ds(peer * depth, depth)], landed.at[j], rs_send.at[j], rs_recv.at[j]
        )
        copy.start()
        scatter.append(copy)
    total = acc[pl.ds(me * depth, depth)]
    for j in range(1, n_lon):
        scatter[j - 1].wait_recv()
        total = total + landed[j]
    mine_out = reduced.at[pl.ds(me * depth, depth)]
    mine_out[...] = total
    gather = []
    for j in range(1, n_lon):
        peer = lax.rem(me + j, n_lon)
        copy = to_lon(peer, mine_out, mine_out, ag_send.at[j], ag_recv.at[j])
        copy.start()
        gather.append(copy)
    for j in range(1, n_lon):
        gather[j - 1].wait_recv()

    sub = lax.broadcasted_iota(jnp.int32, (GROUP, rows), 0)
    for b in range(BASINS):
        above = jnp.zeros((1, rows), F32)
        for g in range(groups):
            x = reduced[g * planes + b]
            for by in (1, 2, 4):
                x = x + jnp.where(sub >= by, pltpu.roll(x, by, 0), 0.0)
            x = x + above
            above = x[GROUP - 1:GROUP]
            zonal[pl.ds((b * groups + g) * GROUP, GROUP), :] = x * scale_layers
    used = BASINS * groups * GROUP
    padded = zonal.shape[0]
    if padded > used:
        zonal[pl.ds(used, padded - used), :] = jnp.zeros((padded - used, rows), F32)
    high, low = split(zonal[...])
    ones = jnp.ones((GROUP, rows), BF16)
    totals[...] = nt_dot(ones, high) + nt_dot(ones, low)
    sends = []
    for j in range(1, n_lat):
        copy = pltpu.make_async_remote_copy(
            src_ref=totals, dst_ref=every.at[j], send_sem=tot_send.at[j], recv_sem=tot_recv.at[j],
            device_id={"lat": lax.rem(me_lat + j, n_lat)}, device_id_type=pl.DeviceIdType.MESH,
        )
        copy.start()
        sends.append(copy)
    upper = (
        lax.broadcasted_iota(jnp.int32, (rows, rows), 0)
        <= lax.broadcasted_iota(jnp.int32, (rows, rows), 1)
    ).astype(F32).astype(BF16)
    running = jnp.dot(high, upper, preferred_element_type=F32) + jnp.dot(
        low, upper, preferred_element_type=F32
    )
    height = groups * GROUP
    for b in range(BASINS):
        stream_out[b] = zonal[pl.ds(b * height, layers), :]
        for g in range(groups):
            size = min(GROUP, layers - g * GROUP)
            heat_out[b, pl.ds(g * GROUP, size), :] = reduced[g * planes + BASINS + b][:size]
    carried = jnp.zeros((GROUP, padded), F32)
    for j in range(1, n_lat):
        sends[j - 1].wait_recv()
        carried = carried + jnp.where(me_lat >= j, every[j], 0.0)
    blocks = []
    for i in range(padded // 128):
        line = carried[0:1, i * 128:(i + 1) * 128]
        blocks.append(jnp.broadcast_to(line, (128, 128)).T)
    spread = jnp.concatenate(blocks, axis=0)
    spread = jnp.concatenate([spread] * (rows // 128), axis=1)
    zonal[...] = (running + spread) * scale_y
    for b in range(BASINS):
        north_out[b] = zonal[pl.ds(b * height, layers), :]

    pl.when(me_lat > 0)(strip_copy.wait_send)
    for copy in scatter + gather + sends:
        copy.wait_send()


def on_device(
    northward_volume_flux, sheet_warmth, ocean_region_ids, ocean_grid_flags, thick_sheet_tally
):
    layers, rows, columns = northward_volume_flux.shape
    n_lat, n_lon = lax.axis_size("lat"), lax.axis_size("lon")
    scales = (
        1.0 / math.sqrt(columns * n_lon), 1.0 / math.sqrt(layers), 1.0 / math.sqrt(rows * n_lat)
    )
    groups = -(-layers // GROUP)
    tiles = groups * 2 * BASINS
    depth = -(-tiles // n_lon)
    padded = -(-BASINS * groups * GROUP // 128) * 128
    out = jax.ShapeDtypeStruct((BASINS, layers, rows), F32)
    anywhere = pl.BlockSpec(memory_space=pl.ANY)
    inside = pl.BlockSpec(memory_space=pltpu.VMEM)
    dma = pltpu.SemaphoreType.DMA
    return pl.pallas_call(
        functools.partial(kernel, n_lat, n_lon, layers, scales),
        out_shape=(out, out, out),
        in_specs=[anywhere, anywhere, inside, inside, inside],
        out_specs=(inside, inside, inside),
        scratch_shapes=[
            pltpu.VMEM((groups * GROUP, rows, columns), BF16),
            pltpu.VMEM((groups * GROUP, rows, columns), BF16),
            pltpu.VMEM((BASINS, rows, columns), BF16),
            pltpu.VMEM((rows, columns), jnp.int32),
            pltpu.VMEM((n_lon * depth, GROUP, rows), F32),
            pltpu.VMEM((n_lon, depth, GROUP, rows), F32),
            pltpu.VMEM((n_lon * depth, GROUP, rows), F32),
            pltpu.VMEM((layers, 8, columns), BF16),
            pltpu.VMEM((padded, rows), F32),
            pltpu.VMEM((GROUP, padded), F32),
            pltpu.VMEM((n_lat, GROUP, padded), F32),
            dma((2, groups)),
            dma((n_lon,)), dma((n_lon,)), dma((n_lon,)), dma((n_lon,)),
            dma, dma,
            dma((n_lat,)), dma((n_lat,)),
        ],
        compiler_params=pltpu.CompilerParams(
            collective_id=0, has_side_effects=True, vmem_limit_bytes=60 * 1024 * 1024
        ),
        name="overturning",
    )(northward_volume_flux, sheet_warmth, ocean_region_ids, ocean_grid_flags, thick_sheet_tally)


def solution(mesh):
    placed = (
        P(None, "lat", "lon"),
        P(None, "lat", "lon"),
        P("lat", "lon"),
        P("lat", "lon"),
        P("lat", "lon"),
    )
    return jax.shard_map(
        on_device,
        mesh=mesh,
        in_specs=placed,
        out_specs=(P(None, None, "lat"), P(None, None, "lat"), P(None, None, "lat")),
        check_vma=False,
    )
```

time: 180 us -> 77.9 us (0.43)
  the two profiles are of different devices: /device:TPU:0 before, /device:TPU:21 now
where the time goes in v1:
time: 77.9 us; the launch traced here: 77.6 us
  Pallas kernels  71.6 us (92%)
  local copies, waits for them, and re-layouts  5.36 us (7%)
    pallas_call x1, Pallas kernels, on_device(): pl.pallas_call(functools.partial(kernel, n_lat, n_lon, layers, scales), o...  71.6 us
    unnamed x3, local copies, waits for them, and re-layouts  5.36 us

profile of v1, /device:TPU:21, one launch (start us, length us, event | category | flops | bytes accessed | tf_op | source)
XLA Modules:
  0.0 77.6 jit_solution(4539358837550284303)
XLA Ops:
  0.6 71.6 %overturning.1 = (f32[5,75,256]{2,1,0:T(8,128)}, f32[5,75,256]{2,1,0:T(8,128)}, f32[5,75,256]{2,1,0:T(8,128)}) custom-call(bf16[75,256,128]{2,1,0:T(8,128)(2,1)} %flux_hbm.1, bf16[75,256,128]{2,1,0:T(8,128)(2,1)} %warm_hbm.1, s32[256,128]{1,0:T(8,128)} %ids_ref.1, s32[256,128]{1,0:T(8,128)} %flags_ref.1, s32[256,128]{1,0:T(8,128)} %tally_ref.1), custom_call_target="tpu_custom_call" | custom-call | tf_op jit(solution)/shard_map/overturning/pallas_call | solution.py:243
  72.2 1.8 %copy.11 = f32[5,75,256]{2,1,0:T(8,128)} copy(f32[5,75,256]{2,1,0:T(8,128)} %get-tuple-element.6) | data formatting | bytes 768000
  74.0 1.8 %copy.12 = f32[5,75,256]{2,1,0:T(8,128)} copy(f32[5,75,256]{2,1,0:T(8,128)} %get-tuple-element.7) | data formatting | bytes 768000
  75.8 1.8 %copy.13 = f32[5,75,256]{2,1,0:T(8,128)} copy(f32[5,75,256]{2,1,0:T(8,128)} %get-tuple-element.8) | data formatting | bytes 768000

commit v2 on v1

--- a/solution.py
+++ b/solution.py
@@ -65,6 +65,7 @@
     if spare:
         flux[pl.ds(layers, spare)] = jnp.zeros((spare, rows, columns), BF16)
         warm[pl.ds(layers, spare)] = jnp.zeros((spare, rows, columns), BF16)
+        strip[pl.ds(layers, spare)] = jnp.zeros((spare, 8, columns), BF16)
     left = acc.shape[0] - groups * planes
     if left:
         acc[pl.ds(groups * planes, left)] = jnp.zeros((left, GROUP, rows), F32)
@@ -73,9 +74,13 @@
         masks[b] = (ids == b).astype(F32).astype(BF16)
     live_tally[...] = flags_ref[...] * tally_ref[...]
 
+    @pl.when(me_lat == n_lat - 1)
+    def _():
+        strip[pl.ds(0, layers)] = jnp.zeros((layers, 8, columns), BF16)
+
     pl.semaphore_wait(barrier, n_lon - 1 + n_lat - 1)
     strip_copy = pltpu.make_async_remote_copy(
-        src_ref=warm_hbm.at[:, pl.ds(0, 8), :], dst_ref=strip,
+        src_ref=warm_hbm.at[:, pl.ds(0, 8), :], dst_ref=strip.at[pl.ds(0, layers)],
         send_sem=strip_send, recv_sem=strip_recv,
         device_id={"lat": lax.rem(me_lat + n_lat - 1, n_lat)},
         device_id_type=pl.DeviceIdType.MESH,
@@ -86,7 +91,31 @@
     lane_half = lax.broadcasted_iota(jnp.int32, (GROUP, 2 * columns), 1) // columns
     slot = lax.broadcasted_iota(jnp.int32, (GROUP, 2 * columns), 0)
 
-    def one_group(g, carry):
+    def to_lon(peer, src, dst, send, recv):
+        return pltpu.make_async_remote_copy(
+            src_ref=src, dst_ref=dst, send_sem=send, recv_sem=recv,
+            device_id={"lon": peer}, device_id_type=pl.DeviceIdType.MESH,
+        )
+
+    scatter = []
+    for j in range(1, n_lon):
+        peer = lax.rem(me + j, n_lon)
+        copy = to_lon(
+            peer, acc.at[pl.ds(peer * depth, depth)], landed.at[j], rs_send.at[j], rs_recv.at[j]
+        )
+        scatter.append(copy)
+    tiles = groups * planes
+    first = lax.rem(me + 1, n_lon) * depth
+    start = jnp.minimum(first, tiles - 1) // planes
+
+    def ready(peer):
+        a = jnp.minimum(peer * depth, tiles - 1) // planes
+        c = jnp.minimum(peer * depth + depth - 1, tiles - 1) // planes
+        cut = jnp.logical_and(a < start, start <= c)
+        return jnp.where(cut, groups - 1, lax.rem(c - start + groups, groups))
+
+    def one_group(step, carry):
+        g = lax.rem(start + step, groups)
         zsum = [jnp.zeros((GROUP, rows), F32) for _ in range(BASINS)]
         hsum = [jnp.zeros((GROUP, rows), F32) for _ in range(BASINS)]
         for pair in range(GROUP // 2):
@@ -97,7 +126,7 @@
                 live = k < live_tally[...]
                 f = jnp.where(live, flux[k].astype(F32), 0.0)
                 t = warm[k].astype(F32)
-                up = jnp.where(last_row, 0.0, pltpu.roll(t, rows - 1, 0))
+                up = jnp.where(last_row, strip[k].astype(F32)[0:1], pltpu.roll(t, rows - 1, 0))
                 high, low = split(f * (t + up))
                 fb = f.astype(BF16)
                 held.append(fb)
@@ -112,46 +141,16 @@
         for b in range(BASINS):
             acc[g * planes + b] = zsum[b] * scale_x
             acc[g * planes + BASINS + b] = hsum[b] * (0.5 * scale_x)
+        for j in range(1, n_lon):
+            pl.when(step == ready(lax.rem(me + j, n_lon)))(scatter[j - 1].start)
         return carry
 
+    pl.when(me_lat < n_lat - 1)(strip_copy.wait_recv)
     for pair in loads:
         for copy in pair:
             copy.wait()
     lax.fori_loop(0, groups, one_group, 0)
 
-    @pl.when(me_lat < n_lat - 1)
-    def _():
-        strip_copy.wait_recv()
-        near = strip[...].astype(F32)[:, 0, :]
-        mine = flux[pl.ds(0, layers), pl.ds(rows - 16, 16), :].astype(F32)[:, 15, :]
-        level = lax.broadcasted_iota(jnp.int32, (layers, columns), 0)
-        tall = live_tally[pl.ds(rows - 1, 1), :]
-        extra = jnp.where(level < tall, near * mine, 0.0) * (0.5 * scale_x)
-        last = ids_ref[pl.ds(rows - 1, 1), :]
-        end = lax.broadcasted_iota(jnp.int32, (GROUP, rows), 1) == rows - 1
-        for b in range(BASINS):
-            column = jnp.sum(jnp.where(last == b, extra, 0.0), axis=1, keepdims=True)
-            if spare:
-                column = jnp.concatenate([column, jnp.zeros((spare, 1), F32)], axis=0)
-            for g in range(groups):
-                at = g * planes + BASINS + b
-                piece = column[g * GROUP:(g + 1) * GROUP]
-                acc[at] = acc[at] + jnp.where(end, piece, 0.0)
-
-    def to_lon(peer, src, dst, send, recv):
-        return pltpu.make_async_remote_copy(
-            src_ref=src, dst_ref=dst, send_sem=send, recv_sem=recv,
-            device_id={"lon": peer}, device_id_type=pl.DeviceIdType.MESH,
-        )
-
-    scatter = []
-    for j in range(1, n_lon):
-        peer = lax.rem(me + j, n_lon)
-        copy = to_lon(
-            peer, acc.at[pl.ds(peer * depth, depth)], landed.at[j], rs_send.at[j], rs_recv.at[j]
-        )
-        copy.start()
-        scatter.append(copy)
     total = acc[pl.ds(me * depth, depth)]
     for j in range(1, n_lon):
         scatter[j - 1].wait_recv()
@@ -253,7 +252,7 @@
             pltpu.VMEM((n_lon * depth, GROUP, rows), F32),
             pltpu.VMEM((n_lon, depth, GROUP, rows), F32),
             pltpu.VMEM((n_lon * depth, GROUP, rows), F32),
-            pltpu.VMEM((layers, 8, columns), BF16),
+            pltpu.VMEM((groups * GROUP, 8, columns), BF16),
             pltpu.VMEM((padded, rows), F32),
             pltpu.VMEM((GROUP, padded), F32),
             pltpu.VMEM((n_lat, GROUP, padded), F32),

time: 77.9 us -> 64.4 us (0.83)
  the two profiles are of different devices: /device:TPU:21 before, /device:TPU:31 now
where the time goes in v2:
time: 64.4 us; the launch traced here: 64.2 us
  Pallas kernels  58.2 us (90%)
  local copies, waits for them, and re-layouts  5.36 us (8%)
    pallas_call x1, Pallas kernels, on_device(): pl.pallas_call(functools.partial(kernel, n_lat, n_lon, layers, scales), o...  58.2 us
    unnamed x3, local copies, waits for them, and re-layouts  5.36 us

profile of v2, /device:TPU:31, one launch (start us, length us, event | category | flops | bytes accessed | tf_op | source)
XLA Modules:
  0.0 64.2 jit_solution(5885786085353325314)
XLA Ops:
  0.6 58.2 %overturning.1 = (f32[5,75,256]{2,1,0:T(8,128)}, f32[5,75,256]{2,1,0:T(8,128)}, f32[5,75,256]{2,1,0:T(8,128)}) custom-call(bf16[75,256,128]{2,1,0:T(8,128)(2,1)} %flux_hbm.1, bf16[75,256,128]{2,1,0:T(8,128)(2,1)} %warm_hbm.1, s32[256,128]{1,0:T(8,128)} %ids_ref.1, s32[256,128]{1,0:T(8,128)} %flags_ref.1, s32[256,128]{1,0:T(8,128)} %tally_ref.1), custom_call_target="tpu_custom_call" | custom-call | tf_op jit(solution)/shard_map/overturning/pallas_call | solution.py:242
  58.8 1.8 %copy.11 = f32[5,75,256]{2,1,0:T(8,128)} copy(f32[5,75,256]{2,1,0:T(8,128)} %get-tuple-element.6) | data formatting | bytes 768000
  60.6 1.8 %copy.12 = f32[5,75,256]{2,1,0:T(8,128)} copy(f32[5,75,256]{2,1,0:T(8,128)} %get-tuple-element.7) | data formatting | bytes 768000
  62.4 1.8 %copy.13 = f32[5,75,256]{2,1,0:T(8,128)} copy(f32[5,75,256]{2,1,0:T(8,128)} %get-tuple-element.8) | data formatting | bytes 768000

commit v3 on v2

--- a/solution.py
+++ b/solution.py
@@ -157,14 +157,35 @@
         total = total + landed[j]
     mine_out = reduced.at[pl.ds(me * depth, depth)]
     mine_out[...] = total
+    half = n_lon // 2
+
+    def lon_at(p):
+        p = lax.rem(p + 2 * n_lon, n_lon)
+        if n_lon % 2:
+            return p
+        return jnp.where(p < half, 2 * p, 2 * (n_lon - 1 - p) + 1)
+
+    spot = me if n_lon % 2 else jnp.where(lax.rem(me, 2) == 0, me // 2, n_lon - 1 - me // 2)
+    pieces = tuple((i * depth // 4, (i + 1) * depth // 4 - i * depth // 4) for i in range(4))
     gather = []
-    for j in range(1, n_lon):
-        peer = lax.rem(me + j, n_lon)
-        copy = to_lon(peer, mine_out, mine_out, ag_send.at[j], ag_recv.at[j])
+    for t in range(half):
+        for c, (at, size) in enumerate(pieces):
+            for way in ((1, -1) if t < n_lon - 1 - half else (1,)):
+                if size == 0:
+                    continue
+                index = (t * 4 + c) * 2 + (way < 0)
+                part = reduced.at[pl.ds(lon_at(spot - way * t) * depth + at, size)]
+                copy = to_lon(lon_at(spot + way), part, part, ag_send.at[index], ag_recv.at[index])
+                gather.append((t, c, way, copy))
+    by_key = {(t, c, way): copy for t, c, way, copy in gather}
+    for t, c, way, copy in gather:
+        if t:
+            by_key[t - 1, c, way].wait_recv()
         copy.start()
-        gather.append(copy)
-    for j in range(1, n_lon):
-        gather[j - 1].wait_recv()
+    for t, c, way, copy in gather:
+        if (t + 1, c, way) not in by_key:
+            copy.wait_recv()
+    gather = [copy for _, _, _, copy in gather]
 
     sub = lax.broadcasted_iota(jnp.int32, (GROUP, rows), 0)
     for b in range(BASINS):
@@ -257,7 +278,7 @@
             pltpu.VMEM((GROUP, padded), F32),
             pltpu.VMEM((n_lat, GROUP, padded), F32),
             dma((2, groups)),
-            dma((n_lon,)), dma((n_lon,)), dma((n_lon,)), dma((n_lon,)),
+            dma((n_lon,)), dma((n_lon,)), dma((4 * n_lon,)), dma((4 * n_lon,)),
             dma, dma,
             dma((n_lat,)), dma((n_lat,)),
         ],

time: 64.4 us -> 63.6 us (0.988)
  the two profiles are of different devices: /device:TPU:31 before, /device:TPU:0 now
where the time goes in v3:
time: 63.6 us; the launch traced here: 63.3 us
  Pallas kernels  57.3 us (90%)
  local copies, waits for them, and re-layouts  5.36 us (8%)
  between operations  0.64 us (1%)
    pallas_call x1, Pallas kernels, on_device(): pl.pallas_call(functools.partial(kernel, n_lat, n_lon, layers, scales), o...  57.3 us
    unnamed x3, local copies, waits for them, and re-layouts  5.36 us

profile of v3, /device:TPU:0, one launch (start us, length us, event | category | flops | bytes accessed | tf_op | source)
XLA Modules:
  0.0 63.3 jit_solution(10983226576595479500)
XLA Ops:
  0.6 57.3 %overturning.1 = (f32[5,75,256]{2,1,0:T(8,128)}, f32[5,75,256]{2,1,0:T(8,128)}, f32[5,75,256]{2,1,0:T(8,128)}) custom-call(bf16[75,256,128]{2,1,0:T(8,128)(2,1)} %flux_hbm.1, bf16[75,256,128]{2,1,0:T(8,128)(2,1)} %warm_hbm.1, s32[256,128]{1,0:T(8,128)} %ids_ref.1, s32[256,128]{1,0:T(8,128)} %flags_ref.1, s32[256,128]{1,0:T(8,128)} %tally_ref.1), custom_call_target="tpu_custom_call" | custom-call | tf_op jit(solution)/shard_map/overturning/pallas_call | solution.py:263
  57.9 1.8 %copy.11 = f32[5,75,256]{2,1,0:T(8,128)} copy(f32[5,75,256]{2,1,0:T(8,128)} %get-tuple-element.6) | data formatting | bytes 768000
  59.7 1.8 %copy.12 = f32[5,75,256]{2,1,0:T(8,128)} copy(f32[5,75,256]{2,1,0:T(8,128)} %get-tuple-element.7) | data formatting | bytes 768000
  61.5 1.8 %copy.13 = f32[5,75,256]{2,1,0:T(8,128)} copy(f32[5,75,256]{2,1,0:T(8,128)} %get-tuple-element.8) | data formatting | bytes 768000
